TPU v7x, 128 devices: a whole 4x4x4 slice. The times are simulated.
128 devices in a mesh: dp: 8 (over y, core), head: 16 (over z, x).
Axes of the slice: x: 4, y: 4, z: 4, core: 2. Of those that a mesh axis runs over, the one named last changes fastest.
Arguments:
- latent: bfloat16 [8192, 1536], P('dp', 'head'), may hold values from -6 to 6
- weight: bfloat16 [1536, 24576], P(None, 'head'), may hold values from -0.15625 to 0.15625
- query_grad: bfloat16 [8192, 24576], P('dp', 'head'), may hold values from -6 to 6
- master: float32 [1536, 24576], P('dp', 'head'), may hold values from -6 to 6
- first_moment: float32 [1536, 24576], P('dp', 'head'), may hold values from -6 to 6
- second_moment: float32 [1536, 24576], P('dp', 'head'), may hold values from 100 to 10000
Outputs:
- queries: bfloat16 [8192, 24576], P('dp', 'head')
- latent_grad: bfloat16 [8192, 1536], P('dp', 'head')
- new_master: float32 [1536, 24576], P('dp', 'head')
- new_first: float32 [1536, 24576], P('dp', 'head')
- new_second: float32 [1536, 24576], P('dp', 'head')
All inputs are finite; a program needn't handle non-finite values.
Results may differ from a plain program's by a relative error of at most 0.014.
Values may be sent and summed in bfloat16 or wider, within the bound.
No kernel may reach another device: no remote copies, remote signals or barrier semaphores. Data moves between devices by JAX's collectives and lax.ppermute only.
A program may use at most 128 MiB of HBM per device.

v0:
```python
import jax
import jax.numpy as jnp
from jax import lax
from jax.sharding import PartitionSpec as P

STEP = 10


def in_blocks(x, dim, length):
    before, after = (x.shape[:dim], x.shape[dim + 1 :])
    return jnp.moveaxis(x.reshape(*before, length, -1, *after), dim, 0)


def sent_and_summed(x, axis, dim):
    length = lax.axis_size(axis)
    blocks = lax.all_to_all(in_blocks(x, dim, length), axis, 0, 0, tiled=True)
    return jnp.sum(blocks.astype(jnp.float32), axis=0)


def on_device(latent, weight, query_grad, master, first_moment, second_moment):
    lat_full = lax.all_gather(latent, "head", axis=1, tiled=True)
    queries = jnp.dot(lat_full, weight, preferred_element_type=jnp.float32).astype(jnp.bfloat16)
    latent_grad = sent_and_summed(
        lax.dot_general(
            weight, query_grad, (((1,), (1,)), ((), ())), preferred_element_type=jnp.float32
        ).astype(jnp.bfloat16),
        "head",
        0,
    ).T.astype(jnp.bfloat16)
    partial_w = lax.dot_general(
        lat_full, query_grad, (((0,), (0,)), ((), ())), preferred_element_type=jnp.float32
    )
    grad = lax.psum_scatter(
        partial_w.astype(jnp.bfloat16), "dp", scatter_dimension=0, tiled=True
    ).astype(jnp.float32)
    new_first = 0.9 * first_moment + 0.1 * grad
    new_second = 0.95 * second_moment + 0.05 * grad * grad
    first_hat = new_first / (1.0 - 0.9**STEP)
    second_hat = new_second / (1.0 - 0.95**STEP)
    new_master = master - 0.01 * (first_hat / (jnp.sqrt(second_hat) + 1e-08) + 0.1 * master)
    return (queries, latent_grad, new_master, new_first, new_second)


def solution(mesh):
    return jax.shard_map(
        on_device,
        mesh=mesh,
        in_specs=(
            P("dp", "head"),
            P(None, "head"),
            P("dp", "head"),
            P("dp", "head"),
            P("dp", "head"),
            P("dp", "head"),
        ),
        out_specs=(
            P("dp", "head"),
            P("dp", "head"),
            P("dp", "head"),
            P("dp", "head"),
            P("dp", "head"),
        ),
        check_vma=False,
    )
```

profile of v0, /device:TPU:0, one launch (start us, length us, event | category | flops | bytes accessed | tf_op | source)
XLA Modules:
  0.0 144.3 jit_solution(5943135301891919004)
XLA Ops:
  7.2 0.0 copy-start
  7.2 0.0 all-gather.2.cloned.1.call-start
  7.2 0.7 all-gather.2.cloned.1.call-update
  7.9 0.0 reduce-scatter.2.cloned.1.call-start
  8.0 52.6 %all-gather.2.cloned.1.call-done = bf16[1024,1536]{0,1:T(8,128)(2,1)} async-done(((bf16[1024,96]{0,1:T(8,128)(2,1)}), bf16[1024,1536]{0,1:T(8,128)(2,1)}) %all-gather.2.cloned.1.call-update) | async-done | bytes 3145744 | tf_op jit(solution)/shard_map/all_gather | solution.py:21
  60.6 0.0 copy-done
  60.6 8.6 %convolution_convert_fusion = bf16[1536,1536]{1,0:T(8,128)(2,1)} fusion(bf16[1024,1536]{0,1:T(8,128)(2,1)} %all-gather.2.cloned.1.call-done, bf16[1024,1536]{1,0:T(8,128)(2,1)S(1)} %copy-done), kind=kOutput, calls=%fused_computation | convolution fusion | flops 4834197504 | bytes 11010048 | tf_op jit(solution)/shard_map/dot_general | solution.py:30
  69.2 0.0 reduce-scatter.2.cloned.1.call-update
  69.2 7.7 %convolution_convert_fusion.1 = bf16[1536,1024]{1,0:T(8,128)(2,1)S(1)} fusion(bf16[1536,1536]{1,0:T(8,128)(2,1)} %param.7, bf16[1024,1536]{1,0:T(8,128)(2,1)S(1)} %copy-done), kind=kOutput, calls=%fused_computation.1 | convolution fusion | flops 4833411072 | bytes 11010048 | tf_op jit(solution)/shard_map/dot_general | solution.py:24
  76.9 43.4 %all_to_all.5 = bf16[16,96,1024]{2,1,0:T(8,128)(2,1)} all-to-all(bf16[16,96,1024]{2,1,0:T(8,128)(2,1)S(1)} %bitcast.8), channel_id=1, replica_groups=mesh['dp'=8,'head'=16] {'head'}, dimensions={0} | all-to-all | bytes 6291456 | tf_op jit(solution)/shard_map/all_to_all | solution.py:16
  120.3 3.3 %reduce_sum.12 = bf16[96,1024]{1,0:T(8,128)(2,1)} reduce(bf16[16,96,1024]{2,1,0:T(8,128)(2,1)} %all_to_all.5, bf16[]{:T(256)} %constant.3.clone.1), dimensions={0}, to_apply=%region_0.0 | reduce | flops 1474560 | bytes 3342338 | tf_op jit(solution)/shard_map/reduce_sum | solution.py:17
  123.6 9.3 %convolution_convert_fusion.2 = bf16[1024,1536]{1,0:T(8,128)(2,1)} fusion(bf16[1024,1536]{0,1:T(8,128)(2,1)} %all-gather.2.cloned.1.call-done, bf16[1536,1536]{1,0:T(8,128)(2,1)} %param.7), kind=kOutput, calls=%fused_computation.2 | convolution fusion | flops 4833411072 | bytes 11010048 | tf_op jit(solution)/shard_map/dot_general | solution.py:22
  132.9 0.0 reduce-scatter.2.cloned.1.call-done
  132.9 4.6 %multiply_subtract_fusion = (f32[192,1536]{1,0:T(8,128)}, f32[192,1536]{1,0:T(8,128)}, f32[192,1536]{1,0:T(8,128)}) fusion(f32[192,1536]{1,0:T(8,128)} %param.9, bf16[192,1536]{1,0:T(8,128)(2,1)} %reduce-scatter.2.cloned.1.call-done, f32[192,1536]{1,0:T(8,128)} %param.10, f32[192,1536]{1,0:T(8,128)} %param.11), kind=kLoop, calls=%fused_computation.7 | loop fusion | flops 4718592 | bytes 7667712 | tf_op jit(solution)/shard_map/sub | solution.py:40
Async XLA Ops:
  7.2 53.4 %copy-start = (bf16[1024,1536]{1,0:T(8,128)(2,1)S(1)}, bf16[1024,1536]{1,0:T(8,128)(2,1)}, u32[]{:S(2)}) copy-start(bf16[1024,1536]{1,0:T(8,128)(2,1)} %param.8) | copy-start | bytes 9437188
  7.2 53.4 %all-gather.2.cloned.1.call-start = ((), (), s32[]{:S(2)}) async-start(), calls=%async_computation.2 | async-start | bytes 3342336 | tf_op jit(solution)/shard_map/all_gather | solution.py:21
  7.9 124.9 %reduce-scatter.2.cloned.1.call-start = ((), (), s32[]{:S(2)}) async-start(), calls=%async_computation.3 | async-start | bytes 5308416 | tf_op jit(solution)/shard_map/reduce_scatter | solution.py:33
Sparse Core Ops, SparseCore 0:
  10.1 50.4 all-gather.1
  69.4 38.2 reduce-scatter.1
where the time goes:
time: 145 us; the launch traced here: 144 us
  waiting for transfers between devices  53.3 us (37%)
  blocking collectives  43.4 us (30%)
  matrix products  25.6 us (18%)
  between operations  14.1 us (10%)
  other arithmetic  7.81 us (5%)
    all_gather x1, waiting for transfers between devices, on_device(): lat_full = lax.all_gather(latent, 'head', axis=1, tiled=True)  52.6 us
    all_to_all x1, blocking collectives, sent_and_summed(): blocks = lax.all_to_all(in_blocks(x, dim, length), axis, 0, 0, tiled=True)  43.4 us
    dot_general x1, matrix products, on_device(): jnp.dot(lat_full, weight, preferred_element_type=jnp.float32)  9.26 us
    dot_general x1, matrix products, on_device(): lax.dot_general(lat_full, query_grad, (((0,), (0,)), ((), ())), preferred...  8.64 us
    dot_general x1, matrix products, on_device(): lax.dot_general(weight, query_grad, (((1,), (1,)), ((), ())), preferred_e...  7.68 us
    sub x1, other arithmetic, on_device(): master - 0.01 * (first_hat / (jnp.sqrt(second_hat) + 1e-08) + 0.1 * master)  4.56 us
    reduce_sum x1, other arithmetic, sent_and_summed(): return jnp.sum(blocks.astype(jnp.float32), axis=0)  3.26 us
  transfers between devices with their start and end apart: 2, of which 1 were waited for; matrix products, arithmetic and copies ran while one was open for 14% of the time, Pallas kernels for 0%

commit v1 on v0

v1 whole, which is shorter than its diff:
```python
import jax
import jax.numpy as jnp
import numpy as np
from jax import lax
from jax.experimental import pallas as pl
from jax.experimental.pallas import tpu as pltpu
from jax.sharding import PartitionSpec as P

STEP = 10
BOTH = ("dp", "head")
B = 96
F32 = jnp.float32
BF16 = jnp.bfloat16
MIB = 1024 * 1024


def device(y, c, z, x):
    return ((y % 4) * 2 + c % 2) * 16 + (z % 4) * 4 + x % 4


def moved(step):
    return [
        (device(y, c, z, x), device(*step(y, c, z, x)))
        for y in range(4)
        for c in range(2)
        for z in range(4)
        for x in range(4)
    ]


def along_a(d):
    return moved(lambda y, c, z, x: (y, c, z, x + d) if c else (y, c, z + d, x))


def along_b(d):
    return moved(lambda y, c, z, x: (y, c, z + d, x) if c else (y, c, z, x + d))


def along_y(d):
    return moved(lambda y, c, z, x: (y + d, c, z, x))


PARTNER = moved(lambda y, c, z, x: (y, 1 - c, z, x))


def sent(x, pairs):
    return lax.ppermute(x, BOTH, pairs)


def indices():
    rows = []
    for dp in range(8):
        for head in range(16):
            y, c, z, x = dp // 2, dp % 2, head // 4, head % 4
            a, b = (x, z) if c else (z, x)

            def at(i, j):
                i, j = i % 4, j % 4
                return 4 * j + i if c else 4 * i + j

            to = [at(a + i, b + j) for i in range(4) for j in range(4)]
            come = [at(a - i, b - j) for i in range(4) for j in range(4)]
            picks = []
            for d in range(4):
                mine = []
                other = []
                for j in (0, 1):
                    u, v = (z - y - d) % 4, (x - 2 * c - j) % 4
                    mine += [v, u] if c else [u, v]
                    other += [u, v] if c else [v, u]
                picks += mine + other
            rows.append(to + come + picks)
    return np.array(rows, np.int32)


TABLE = indices()


def lat_grad_kernel(idx, w0, w1, w2, w3, g, *outs):
    w = jnp.concatenate([w0[...], w1[...], w2[...], w3[...]], axis=0)
    r = lax.dot_general(w, g[...], (((1,), (1,)), ((), ())), preferred_element_type=F32)
    for k, out in enumerate(outs):

        @pl.when(pl.program_id(0) == k)
        def _():
            out[...] = r.astype(BF16)


def lat_grad_parts(weight, query_grad, heads):
    return pl.pallas_call(
        lat_grad_kernel,
        grid_spec=pltpu.PrefetchScalarGridSpec(
            num_scalar_prefetch=1,
            grid=(2,),
            in_specs=[pl.BlockSpec((B, 1536), lambda d, idx, j=j: (idx[d * 4 + j], 0)) for j in range(4)]
            + [pl.BlockSpec((1024, 1536), lambda d, idx: (0, 0))],
            out_specs=[pl.BlockSpec((4 * B, 1024), lambda d, idx: (0, 0))] * 2,
        ),
        out_shape=[jax.ShapeDtypeStruct((4 * B, 1024), BF16)] * 2,
        compiler_params=pltpu.CompilerParams(vmem_limit_bytes=24 * MIB),
        cost_estimate=pl.CostEstimate(flops=1024 * 1536 * 1536, bytes_accessed=6000000, transcendentals=0),
    )(heads, weight, weight, weight, weight, query_grad)


def assemble_kernel(idx, s0, s1, s2, s3, full):
    for k2, src in enumerate((s0, s1, s2, s3)):
        for k1 in range(4):
            full[idx[k2 * 4 + k1]] = src[k1]


def assembled(pieces, idx):
    return pl.pallas_call(
        assemble_kernel,
        grid_spec=pltpu.PrefetchScalarGridSpec(
            num_scalar_prefetch=1,
            grid=(),
            in_specs=[pl.BlockSpec(memory_space=pltpu.VMEM)] * 4,
            out_specs=pl.BlockSpec(memory_space=pltpu.VMEM),
        ),
        out_shape=jax.ShapeDtypeStruct((16, B, 1024), BF16),
        compiler_params=pltpu.CompilerParams(vmem_limit_bytes=8 * MIB),
        cost_estimate=pl.CostEstimate(flops=0, bytes_accessed=6000000, transcendentals=0),
        name="assemble",
    )(idx, *pieces)


def w_grad_kernel(idx, *refs):
    pieces = (refs[:4], refs[4:8])
    q, q_other, out0, out1, lhs = refs[8:]

    @pl.when(pl.program_id(0) == 0)
    def _():
        for side in range(2):
            for j in range(4):
                at = (j // 2) * 8 + side * 4 + (j % 2) * 2
                for k2 in range(4):

                    @pl.when(idx[at] == k2)
                    def _():
                        lhs[side, j * B : (j + 1) * B] = pieces[side][k2][idx[at + 1]]

    r = jnp.dot(lhs[0], q[...], preferred_element_type=F32)
    r += jnp.dot(lhs[1], q_other[...], preferred_element_type=F32)
    r = r.astype(BF16)
    out0[...] = r[:192]
    out1[...] = r[192:]


def w_grad_parts(own, other, g, g_other, picks):
    n = 3
    return pl.pallas_call(
        w_grad_kernel,
        grid_spec=pltpu.PrefetchScalarGridSpec(
            num_scalar_prefetch=1,
            grid=(n,),
            in_specs=[pl.BlockSpec(memory_space=pltpu.VMEM)] * 8
            + [pl.BlockSpec((1024, 1536 // n), lambda t, idx: (0, t))] * 2,
            out_specs=[pl.BlockSpec((192, 1536 // n), lambda t, idx: (0, t))] * 2,
            scratch_shapes=[pltpu.VMEM((2, 384, 1024), BF16)],
        ),
        out_shape=[jax.ShapeDtypeStruct((192, 1536), BF16)] * 2,
        compiler_params=pltpu.CompilerParams(vmem_limit_bytes=24 * MIB),
        cost_estimate=pl.CostEstimate(flops=2 * 384 * 2048 * 1536, bytes_accessed=9000000, transcendentals=0),
    )(picks, *own, *other, g, g_other)


def update(grad, master, first_moment, second_moment):
    new_first = 0.9 * first_moment + 0.1 * grad
    new_second = 0.95 * second_moment + 0.05 * grad * grad
    first_hat = new_first / (1.0 - 0.9**STEP)
    second_hat = new_second / (1.0 - 0.95**STEP)
    new_master = master - 0.01 * (first_hat / (jnp.sqrt(second_hat) + 1e-08) + 0.1 * master)
    return new_master, new_first, new_second


def sends(blocks, pairs, steps=(1, 2, 3)):
    out = {}
    for d in steps:
        out[d] = sent(blocks(d), pairs(d))
    return out


def pick(table, *spans):
    return jnp.concatenate([table[i:j] for i, j in spans])


def on_device(latent, weight, query_grad, master, first_moment, second_moment):
    table = lax.dynamic_slice(jnp.asarray(TABLE), (lax.axis_index("dp") * 16 + lax.axis_index("head"), 0), (1, 64))[0]

    own = latent.T
    near = sends(lambda d: own, along_b)
    g_other = sent(query_grad, PARTNER)
    row = jnp.stack([own, near[1], near[2], near[3]])
    rows = {0: row, **sends(lambda d: row, along_a)}
    parts = {}
    parts[1], parts[3] = lat_grad_parts(weight, query_grad, pick(table, (4, 8), (12, 16)))
    parts[2], parts[0] = lat_grad_parts(weight, query_grad, pick(table, (8, 12), (0, 4)))
    got = sends(lambda d: parts[d], along_a)
    others = sends(lambda d: rows[d], lambda d: PARTNER, (0, 1, 3, 2))

    mine = [rows[d] for d in range(4)]
    theirs = [others[d] for d in range(4)]
    sums = {}
    sums[1], sums[3] = w_grad_parts(mine, theirs, query_grad, g_other, pick(table, (40, 48), (56, 64)))
    sums[2], sums[0] = w_grad_parts(mine, theirs, query_grad, g_other, pick(table, (48, 56), (32, 40)))
    come = sends(lambda d: sums[d], along_y)

    half = (parts[0].astype(F32) + got[1].astype(F32)) + (got[2].astype(F32) + got[3].astype(F32))
    half = half.astype(BF16).reshape(4, B, 1024)
    final = sends(lambda d: half[d], along_b)

    full = assembled(mine, table[16:32]).reshape(1536, 1024)
    queries = lax.dot_general(full, weight, (((0,), (0,)), ((), ())), preferred_element_type=F32).astype(BF16)
    latent_grad = sum(p.astype(F32) for p in (half[0], final[1], final[2], final[3])).astype(BF16).T
    grad = sum(s.astype(F32) for s in (sums[0], come[1], come[2], come[3]))
    return (queries, latent_grad, *update(grad, master, first_moment, second_moment))


def solution(mesh):
    spec = P("dp", "head")
    return jax.shard_map(
        on_device,
        mesh=mesh,
        in_specs=(spec, P(None, "head"), spec, spec, spec, spec),
        out_specs=(spec,) * 5,
        check_vma=False,
    )
```

time: 145 us -> 111 us (0.77)
  blocking collectives: 43.4 us -> 0 us
  starting transfers between devices: 0.08 us -> 30.7 us
  matrix products: 25.6 us -> 6.69 us
  Pallas kernels: 0 us -> 16.6 us
  between operations: 14.1 us -> 0.74 us
  waiting for transfers between devices: 53.3 us -> 46.5 us
  local copies, waits for them, and re-layouts: 0.01 us -> 5.21 us
  other arithmetic: 7.81 us -> 4.26 us
    all_gather x1 -> x0, waiting for transfers between devices: 52.6 us -> none  [on_device(): lat_full = lax.all_gather(latent, 'head', axis=1, tiled=True)]
    ppermute x0 -> x20, waiting for transfers between devices: none -> 46.5 us  [sent(): return lax.ppermute(x, BOTH, pairs)]
    all_to_all x1 -> x0, blocking collectives: 43.4 us -> none  [sent_and_summed(): blocks = lax.all_to_all(in_blocks(x, dim, length), axis, 0, 0, tiled=True)]
    ppermute x0 -> x20, starting transfers between devices: none -> 30.7 us  [sent(): return lax.ppermute(x, BOTH, pairs)]
    dot_general x3 -> x1, matrix products: 25.6 us -> 6.69 us  [on_device(): lax.dot_general(full, weight, (((0,), (0,)), ((), ())), preferred_element...]
    pallas_call x0 -> x5, Pallas kernels: none -> 16.6 us  [the longest x2 8.76 us: w_grad_parts(): pl.pallas_call(w_grad_kernel, grid_spec=pltpu.PrefetchScalarGridSpec(num_...]
    unnamed x2 -> x16, local copies, waits for them, and re-layouts: 0.01 us -> 4.25 us
    reduce_sum x1 -> x0, other arithmetic: 3.26 us -> none  [sent_and_summed(): return jnp.sum(blocks.astype(jnp.float32), axis=0)]
  transfers between devices with their start and end apart: 2 -> 20, of which waited for: 1 -> 9; matrix products, arithmetic and copies ran while one was open for 14% -> 8% of each run, Pallas kernels for 0% -> 15%
where the time goes in v1:
time: 111 us
  waiting for transfers between devices  46.5 us (42%)
  starting transfers between devices  30.7 us (28%)
  Pallas kernels  16.6 us (15%)
  matrix products  6.69 us (6%)
  local copies, waits for them, and re-layouts  5.21 us (5%)
  other arithmetic  4.26 us (4%)
    ppermute x20, waiting for transfers between devices, sent(): return lax.ppermute(x, BOTH, pairs)  46.5 us
    ppermute x20, starting transfers between devices, sent(): return lax.ppermute(x, BOTH, pairs)  30.7 us
    pallas_call x2, Pallas kernels, w_grad_parts(): pl.pallas_call(w_grad_kernel, grid_spec=pltpu.PrefetchScalarGridSpec(num_...  8.76 us
    pallas_call x2, Pallas kernels, lat_grad_parts(): pl.pallas_call(lat_grad_kernel, grid_spec=pltpu.PrefetchScalarGridSpec(nu...  7.08 us
    dot_general x1, matrix products, on_device(): lax.dot_general(full, weight, (((0,), (0,)), ((), ())), preferred_element...  6.69 us
    unnamed x16, local copies, waits for them, and re-layouts  4.25 us
    sub x1, other arithmetic, update(): master - 0.01 * (first_hat / (jnp.sqrt(second_hat) + 1e-08) + 0.1 * master)  2.58 us
  transfers between devices with their start and end apart: 20, of which 9 were waited for; matrix products, arithmetic and copies ran while one was open for 8% of the time, Pallas kernels for 15%

profile of v1, /device:TPU:0, one launch (start us, length us, event | category | flops | bytes accessed | tf_op | source)
XLA Modules:
  0.0 110.7 jit_solution(4738233794303131059)
XLA Ops:
  1.6 2.3 %copy-done = bf16[1536,1536]{1,0:T(8,128)(2,1)S(1)} copy-done((bf16[1536,1536]{1,0:T(8,128)(2,1)S(1)}, bf16[1536,1536]{1,0:T(8,128)(2,1)}, u32[]{:S(2)}) %copy-start) | copy-done | bytes 4718616
  3.9 1.9 %copy-done.2 = bf16[1024,1536]{1,0:T(8,128)(2,1)S(1)} copy-done((bf16[1024,1536]{1,0:T(8,128)(2,1)S(1)}, bf16[1024,1536]{1,0:T(8,128)(2,1)}, u32[]{:S(2)}) %copy-start.2) | copy-done | bytes 3145752
  5.8 3.5 %shard_map.111 = (bf16[384,1024]{1,0:T(8,128)(2,1)S(1)}, bf16[384,1024]{1,0:T(8,128)(2,1)S(1)}) custom-call(s32[8]{0:T(128)S(1)} %get-tuple-element.36.idx, bf16[1536,1536]{1,0:T(8,128)(2,1)S(1)} %copy-done, bf16[1536,1536]{1,0:T(8,128)(2,1)S(1)} %copy-done, bf16[1536,1536]{1,0:T(8,128)(2,1)S(1)} %copy-done, bf16[1536,1536]{1,0:T(8,128)(2,1)S(1)} %copy-done, ...), custom_call_target="tpu_custom_call" | custom-call | flops 2415919104 | bytes 6000000 | tf_op jit(solution)/shard_map/pallas_call | solution.py:90
  9.4 2.1 %collective-permute-start.6 = (bf16[384,1024]{1,0:T(8,128)(2,1)S(1)}, bf16[384,1024]{1,0:T(8,128)(2,1)S(1)}, u32[]{:S(2)}, u32[]{:S(2)}) collective-permute-start(bf16[384,1024]{1,0:T(8,128)(2,1)S(1)} %get-tuple-element.14), channel_id=1, source_target_pairs={{0,4},{1,5},{2,6},{3,7},{4,8},{5,9},{6,10},{7,11},{8,12},{9,13},{1... | collective-permute-start | bytes 2359304 | tf_op jit(solution)/shard_map/ppermute | solution.py:47
  11.5 3.5 %shard_map.110 = (bf16[384,1024]{1,0:T(8,128)(2,1)S(1)}, bf16[384,1024]{1,0:T(8,128)(2,1)S(1)}) custom-call(s32[8]{0:T(128)S(1)} %get-tuple-element.35.idx, bf16[1536,1536]{1,0:T(8,128)(2,1)S(1)} %copy-done.1, bf16[1536,1536]{1,0:T(8,128)(2,1)S(1)} %copy-done.1, bf16[1536,1536]{1,0:T(8,128)(2,1)S(1)} %copy-done.1, bf16[1536,1536]{1,0:T(8,128)(2,1)S(1)} %copy-done.1, ...), custom_call_target="tpu_custom_call" | custom-call | flops 2415919104 | bytes 6000000 | tf_op jit(solution)/shard_map/pallas_call | solution.py:90
  15.0 3.7 %collective-permute-start.7 = (bf16[384,1024]{1,0:T(8,128)(2,1)S(1)}, bf16[384,1024]{1,0:T(8,128)(2,1)S(1)}, u32[]{:S(2)}, u32[]{:S(2)}) collective-permute-start(bf16[384,1024]{1,0:T(8,128)(2,1)S(1)} %get-tuple-element.15), channel_id=1, source_target_pairs={{0,8},{1,9},{2,10},{3,11},{4,12},{5,13},{6,14},{7,15},{8,0},{9,1},... | collective-permute-start | bytes 2359304 | tf_op jit(solution)/shard_map/ppermute | solution.py:47
  18.7 1.5 %collective-permute-start = (bf16[96,1024]{1,0:T(8,128)(2,1)S(1)}, bf16[96,1024]{1,0:T(8,128)(2,1)S(1)}, u32[]{:S(2)}, u32[]{:S(2)}) collective-permute-start(bf16[96,1024]{1,0:T(8,128)(2,1)S(1)} %bitcast.30), channel_id=1, source_target_pairs={{0,1},{1,2},{2,3},{3,0},{4,5},{5,6},{6,7},{7,4},{8,9},{9,10},{10,1... | collective-permute-start | bytes 589832 | tf_op jit(solution)/shard_map/ppermute | solution.py:47
  20.2 2.7 %collective-permute-start.1 = (bf16[96,1024]{1,0:T(8,128)(2,1)S(1)}, bf16[96,1024]{1,0:T(8,128)(2,1)S(1)}, u32[]{:S(2)}, u32[]{:S(2)}) collective-permute-start(bf16[96,1024]{1,0:T(8,128)(2,1)S(1)} %bitcast.31), channel_id=1, source_target_pairs={{0,2},{1,3},{2,0},{3,1},{4,6},{5,7},{6,4},{7,5},{8,10},{9,11},{10,... | collective-permute-start | bytes 589832 | tf_op jit(solution)/shard_map/ppermute | solution.py:47
  22.9 5.7 %collective-permute-done = bf16[96,1024]{1,0:T(8,128)(2,1)S(1)} collective-permute-done((bf16[96,1024]{1,0:T(8,128)(2,1)S(1)}, bf16[96,1024]{1,0:T(8,128)(2,1)S(1)}, u32[]{:S(2)}, u32[]{:S(2)}) %collective-permute-start) | collective-permute-done | bytes 196640 | tf_op jit(solution)/shard_map/ppermute | solution.py:47
  29.2 3.6 %collective-permute-done.1 = bf16[96,1024]{1,0:T(8,128)(2,1)S(1)} collective-permute-done((bf16[96,1024]{1,0:T(8,128)(2,1)S(1)}, bf16[96,1024]{1,0:T(8,128)(2,1)S(1)}, u32[]{:S(2)}, u32[]{:S(2)}) %collective-permute-start.1) | collective-permute-done | bytes 196640 | tf_op jit(solution)/shard_map/ppermute | solution.py:47
  38.0 9.0 %collective-permute-done.8 = bf16[384,1024]{1,0:T(8,128)(2,1)S(1)} collective-permute-done((bf16[384,1024]{1,0:T(8,128)(2,1)S(1)}, bf16[384,1024]{1,0:T(8,128)(2,1)S(1)}, u32[]{:S(2)}, u32[]{:S(2)}) %collective-permute-start.8) | collective-permute-done | bytes 786464 | tf_op jit(solution)/shard_map/ppermute | solution.py:47
  47.0 9.2 %collective-permute-done.3.s1.refs_1_ = bf16[4,96,1024]{2,1,0:T(8,128)(2,1)S(1)} collective-permute-done((bf16[4,96,1024]{2,1,0:T(8,128)(2,1)S(1)}, bf16[4,96,1024]{2,1,0:T(8,128)(2,1)S(1)}, u32[]{:S(2)}, u32[]{:S(2)}) %collective-permute-start.3) | collective-permute-done | bytes 786464 | tf_op jit(solution)/shard_map/ppermute | solution.py:47
  56.1 5.3 %collective-permute-start.13 = (bf16[4,96,1024]{2,1,0:T(8,128)(2,1)S(1)}, bf16[4,96,1024]{2,1,0:T(8,128)(2,1)S(1)}, u32[]{:S(2)}, u32[]{:S(2)}) collective-permute-start(bf16[4,96,1024]{2,1,0:T(8,128)(2,1)S(1)} %collective-permute-done.3.s1.refs_1_), channel_id=1, source_target_pairs={{0,16},{1,17},{2,18},{3,19},{4,20},{5,21},{6,22},{7,23},{8,24},{9,... | collective-permute-start | bytes 2359304 | tf_op jit(solution)/shard_map/ppermute | solution.py:47
  61.5 2.4 %collective-permute-done.5.s3.refs_3_ = bf16[4,96,1024]{2,1,0:T(8,128)(2,1)S(1)} collective-permute-done((bf16[4,96,1024]{2,1,0:T(8,128)(2,1)S(1)}, bf16[4,96,1024]{2,1,0:T(8,128)(2,1)S(1)}, u32[]{:S(2)}, u32[]{:S(2)}) %collective-permute-start.5) | collective-permute-done | bytes 786464 | tf_op jit(solution)/shard_map/ppermute | solution.py:47
  65.4 3.4 %collective-permute-start.10 = (bf16[96,1024]{1,0:T(8,128)(2,1)S(1)}, bf16[96,1024]{1,0:T(8,128)(2,1)S(1)}, u32[]{:S(2)}, u32[]{:S(2)}) collective-permute-start(bf16[96,1024]{1,0:T(8,128)(2,1)S(1)} %get-tuple-element.26), channel_id=1, source_target_pairs={{0,2},{1,3},{2,0},{3,1},{4,6},{5,7},{6,4},{7,5},{8,10},{9,11},{10,... | collective-permute-start | bytes 589832 | tf_op jit(solution)/shard_map/ppermute | solution.py:47
  69.4 1.4 %collective-permute-start.9 = (bf16[96,1024]{1,0:T(8,128)(2,1)S(1)}, bf16[96,1024]{1,0:T(8,128)(2,1)S(1)}, u32[]{:S(2)}, u32[]{:S(2)}) collective-permute-start(bf16[96,1024]{1,0:T(8,128)(2,1)S(1)} %get-tuple-element.24), channel_id=1, source_target_pairs={{0,1},{1,2},{2,3},{3,0},{4,5},{5,6},{6,7},{7,4},{8,9},{9,10},{10,1... | collective-permute-start | bytes 589832 | tf_op jit(solution)/shard_map/ppermute | solution.py:47
  70.8 4.4 %shard_map.113 = (bf16[192,1536]{1,0:T(8,128)(2,1)S(1)}, bf16[192,1536]{1,0:T(8,128)(2,1)S(1)}) custom-call(s32[16]{0:T(128)S(1)} %get-tuple-element.38.idx, bf16[4,96,1024]{2,1,0:T(8,128)(2,1)S(1)} %pad_maximum_fusion.s0.refs_0_, bf16[4,96,1024]{2,1,0:T(8,128)(2,1)S(1)} %collective-permute-done.3.s1.refs_1_, ...), custom_call_target="tpu_custom_call" | custom-call | flops 2415919104 | bytes 9000000 | tf_op jit(solution)/shard_map/pallas_call | solution.py:151
  75.2 1.6 %collective-permute-start.17 = (bf16[192,1536]{1,0:T(8,128)(2,1)S(1)}, bf16[192,1536]{1,0:T(8,128)(2,1)S(1)}, u32[]{:S(2)}, u32[]{:S(2)}) collective-permute-start(bf16[192,1536]{1,0:T(8,128)(2,1)S(1)} %get-tuple-element.18), channel_id=1, source_target_pairs={{0,32},{1,33},{2,34},{3,35},{4,36},{5,37},{6,38},{7,39},{8,40},{9,... | collective-permute-start | bytes 1769480 | tf_op jit(solution)/shard_map/ppermute | solution.py:47
  76.9 4.4 %shard_map.112 = (bf16[192,1536]{1,0:T(8,128)(2,1)S(1)}, bf16[192,1536]{1,0:T(8,128)(2,1)S(1)}) custom-call(s32[16]{0:T(128)S(1)} %get-tuple-element.37.idx, bf16[4,96,1024]{2,1,0:T(8,128)(2,1)S(1)} %pad_maximum_fusion.s0.refs_0_, bf16[4,96,1024]{2,1,0:T(8,128)(2,1)S(1)} %collective-permute-done.3.s1.refs_1_, ...), custom_call_target="tpu_custom_call" | custom-call | flops 2415919104 | bytes 9000000 | tf_op jit(solution)/shard_map/pallas_call | solution.py:151
  81.3 3.2 %collective-permute-start.18 = (bf16[192,1536]{1,0:T(8,128)(2,1)S(1)}, bf16[192,1536]{1,0:T(8,128)(2,1)S(1)}, u32[]{:S(2)}, u32[]{:S(2)}) collective-permute-start(bf16[192,1536]{1,0:T(8,128)(2,1)S(1)} %get-tuple-element.19), channel_id=1, source_target_pairs={{0,64},{1,65},{2,66},{3,67},{4,68},{5,69},{6,70},{7,71},{8,72},{9,... | collective-permute-start | bytes 1769480 | tf_op jit(solution)/shard_map/ppermute | solution.py:47
  85.8 6.7 %convolution_convert_fusion = bf16[1024,1536]{1,0:T(8,128)(2,1)} fusion(bf16[1536,1024]{1,0:T(8,128)(2,1)S(1)} %bitcast.29, bf16[1536,1536]{1,0:T(8,128)(2,1)S(1)} %copy-done.1), kind=kOutput, calls=%fused_computation | convolution fusion | flops 4833411072 | bytes 11010048 | tf_op jit(solution)/shard_map/dot_general | solution.py:213
  93.3 10.7 %collective-permute-done.18 = bf16[192,1536]{1,0:T(8,128)(2,1)S(1)} collective-permute-done((bf16[192,1536]{1,0:T(8,128)(2,1)S(1)}, bf16[192,1536]{1,0:T(8,128)(2,1)S(1)}, u32[]{:S(2)}, u32[]{:S(2)}) %collective-permute-start.18) | collective-permute-done | bytes 589856 | tf_op jit(solution)/shard_map/ppermute | solution.py:47
  104.0 4.1 %collective-permute-done.19 = bf16[192,1536]{1,0:T(8,128)(2,1)S(1)} collective-permute-done((bf16[192,1536]{1,0:T(8,128)(2,1)S(1)}, bf16[192,1536]{1,0:T(8,128)(2,1)S(1)}, u32[]{:S(2)}, u32[]{:S(2)}) %collective-permute-start.19) | collective-permute-done | bytes 589856 | tf_op jit(solution)/shard_map/ppermute | solution.py:47
  108.1 2.6 %multiply_subtract_fusion = (f32[192,1536]{1,0:T(8,128)}, f32[192,1536]{1,0:T(8,128)}, f32[192,1536]{1,0:T(8,128)}) fusion(f32[192,1536]{1,0:T(8,128)S(1)} %copy-done.4, bf16[192,1536]{1,0:T(8,128)(2,1)S(1)} %collective-permute-done.19, bf16[192,1536]{1,0:T(8,128)(2,1)S(1)} %collective-permute-done.18, bf16[192,1536]{1,0:T(8,128)(2,1)S(1)} %collective-permute-done.17, ...), kind=kLoop, calls=%fused_computation.4 | loop fusion | flops 6488064 | bytes 9437184 | tf_op jit(solution)/shard_map/sub | solution.py:172
  (49 shorter events, 10.9 us)
Async XLA Ops:
  0.6 70.2 %collective-permute-start.16 = (bf16[1024,1536]{1,0:T(8,128)(2,1)}, bf16[1024,1536]{1,0:T(8,128)(2,1)S(1)}, u32[]{:S(2)}, u32[]{:S(2)}) collective-permute-start(bf16[1024,1536]{1,0:T(8,128)(2,1)} %refs_8_.3), channel_id=1, source_target_pairs={{0,16},{1,17},{2,18},{3,19},{4,20},{5,21},{6,22},{7,23},{8,24},{9,... | collective-permute-start | bytes 9437192 | tf_op jit(solution)/shard_map/ppermute | solution.py:47
  9.4 25.7 %collective-permute-start.6 = (bf16[384,1024]{1,0:T(8,128)(2,1)S(1)}, bf16[384,1024]{1,0:T(8,128)(2,1)S(1)}, u32[]{:S(2)}, u32[]{:S(2)}) collective-permute-start(bf16[384,1024]{1,0:T(8,128)(2,1)S(1)} %get-tuple-element.14), channel_id=1, source_target_pairs={{0,4},{1,5},{2,6},{3,7},{4,8},{5,9},{6,10},{7,11},{8,12},{9,13},{1... | collective-permute-start | bytes 2359304 | tf_op jit(solution)/shard_map/ppermute | solution.py:47
  11.5 7.2 %copy-start.7 = (bf16[1024,96]{0,1:T(8,128)(2,1)S(1)}, bf16[1024,96]{0,1:T(8,128)(2,1)}, u32[]{:S(2)}) copy-start(bf16[1024,96]{0,1:T(8,128)(2,1)} %param.7) | copy-start | bytes 589828
  15.0 22.6 %collective-permute-start.7 = (bf16[384,1024]{1,0:T(8,128)(2,1)S(1)}, bf16[384,1024]{1,0:T(8,128)(2,1)S(1)}, u32[]{:S(2)}, u32[]{:S(2)}) collective-permute-start(bf16[384,1024]{1,0:T(8,128)(2,1)S(1)} %get-tuple-element.15), channel_id=1, source_target_pairs={{0,8},{1,9},{2,10},{3,11},{4,12},{5,13},{6,14},{7,15},{8,0},{9,1},... | collective-permute-start | bytes 2359304 | tf_op jit(solution)/shard_map/ppermute | solution.py:47
  18.7 10.0 %collective-permute-start = (bf16[96,1024]{1,0:T(8,128)(2,1)S(1)}, bf16[96,1024]{1,0:T(8,128)(2,1)S(1)}, u32[]{:S(2)}, u32[]{:S(2)}) collective-permute-start(bf16[96,1024]{1,0:T(8,128)(2,1)S(1)} %bitcast.30), channel_id=1, source_target_pairs={{0,1},{1,2},{2,3},{3,0},{4,5},{5,6},{6,7},{7,4},{8,9},{9,10},{10,1... | collective-permute-start | bytes 589832 | tf_op jit(solution)/shard_map/ppermute | solution.py:47
  20.2 12.7 %collective-permute-start.1 = (bf16[96,1024]{1,0:T(8,128)(2,1)S(1)}, bf16[96,1024]{1,0:T(8,128)(2,1)S(1)}, u32[]{:S(2)}, u32[]{:S(2)}) collective-permute-start(bf16[96,1024]{1,0:T(8,128)(2,1)S(1)} %bitcast.31), channel_id=1, source_target_pairs={{0,2},{1,3},{2,0},{3,1},{4,6},{5,7},{6,4},{7,5},{8,10},{9,11},{10,... | collective-permute-start | bytes 589832 | tf_op jit(solution)/shard_map/ppermute | solution.py:47
  28.7 5.7 %collective-permute-start.2 = (bf16[96,1024]{1,0:T(8,128)(2,1)S(1)}, bf16[96,1024]{1,0:T(8,128)(2,1)S(1)}, u32[]{:S(2)}, u32[]{:S(2)}) collective-permute-start(bf16[96,1024]{1,0:T(8,128)(2,1)S(1)} %bitcast.32), channel_id=1, source_target_pairs={{0,3},{1,0},{2,1},{3,2},{4,7},{5,4},{6,5},{7,6},{8,11},{9,8},{10,9... | collective-permute-start | bytes 589832 | tf_op jit(solution)/shard_map/ppermute | solution.py:47
  32.9 14.1 %collective-permute-start.8 = (bf16[384,1024]{1,0:T(8,128)(2,1)S(1)}, bf16[384,1024]{1,0:T(8,128)(2,1)S(1)}, u32[]{:S(2)}, u32[]{:S(2)}) collective-permute-start(bf16[384,1024]{1,0:T(8,128)(2,1)S(1)} %get-tuple-element.16), channel_id=1, source_target_pairs={{0,12},{1,13},{2,14},{3,15},{4,0},{5,1},{6,2},{7,3},{8,4},{9,5},{1... | collective-permute-start | bytes 2359304 | tf_op jit(solution)/shard_map/ppermute | solution.py:47
  34.4 21.7 %collective-permute-start.3 = (bf16[4,96,1024]{2,1,0:T(8,128)(2,1)S(1)}, bf16[4,96,1024]{2,1,0:T(8,128)(2,1)S(1)}, u32[]{:S(2)}, u32[]{:S(2)}) collective-permute-start(bf16[4,96,1024]{2,1,0:T(8,128)(2,1)S(1)} %pad_maximum_fusion.s0.refs_0_), channel_id=1, source_target_pairs={{0,4},{1,5},{2,6},{3,7},{4,8},{5,9},{6,10},{7,11},{8,12},{9,13},{1... | collective-permute-start | bytes 2359304 | tf_op jit(solution)/shard_map/ppermute | solution.py:47
  35.1 26.4 %collective-permute-start.4 = (bf16[4,96,1024]{2,1,0:T(8,128)(2,1)S(1)}, bf16[4,96,1024]{2,1,0:T(8,128)(2,1)S(1)}, u32[]{:S(2)}, u32[]{:S(2)}) collective-permute-start(bf16[4,96,1024]{2,1,0:T(8,128)(2,1)S(1)} %pad_maximum_fusion.s0.refs_0_), channel_id=1, source_target_pairs={{0,8},{1,9},{2,10},{3,11},{4,12},{5,13},{6,14},{7,15},{8,0},{9,1},... | collective-permute-start | bytes 2359304 | tf_op jit(solution)/shard_map/ppermute | solution.py:47
  37.7 26.2 %collective-permute-start.5 = (bf16[4,96,1024]{2,1,0:T(8,128)(2,1)S(1)}, bf16[4,96,1024]{2,1,0:T(8,128)(2,1)S(1)}, u32[]{:S(2)}, u32[]{:S(2)}) collective-permute-start(bf16[4,96,1024]{2,1,0:T(8,128)(2,1)S(1)} %pad_maximum_fusion.s0.refs_0_), channel_id=1, source_target_pairs={{0,12},{1,13},{2,14},{3,15},{4,0},{5,1},{6,2},{7,3},{8,4},{9,5},{1... | collective-permute-start | bytes 2359304 | tf_op jit(solution)/shard_map/ppermute | solution.py:47
  47.0 18.4 %collective-permute-start.12 = (bf16[4,96,1024]{2,1,0:T(8,128)(2,1)S(1)}, bf16[4,96,1024]{2,1,0:T(8,128)(2,1)S(1)}, u32[]{:S(2)}, u32[]{:S(2)}) collective-permute-start(bf16[4,96,1024]{2,1,0:T(8,128)(2,1)S(1)} %pad_maximum_fusion.s0.refs_0_), channel_id=1, source_target_pairs={{0,16},{1,17},{2,18},{3,19},{4,20},{5,21},{6,22},{7,23},{8,24},{9,... | collective-permute-start | bytes 2359304 | tf_op jit(solution)/shard_map/ppermute | solution.py:47
  56.1 12.7 %collective-permute-start.13 = (bf16[4,96,1024]{2,1,0:T(8,128)(2,1)S(1)}, bf16[4,96,1024]{2,1,0:T(8,128)(2,1)S(1)}, u32[]{:S(2)}, u32[]{:S(2)}) collective-permute-start(bf16[4,96,1024]{2,1,0:T(8,128)(2,1)S(1)} %collective-permute-done.3.s1.refs_1_), channel_id=1, source_target_pairs={{0,16},{1,17},{2,18},{3,19},{4,20},{5,21},{6,22},{7,23},{8,24},{9,... | collective-permute-start | bytes 2359304 | tf_op jit(solution)/shard_map/ppermute | solution.py:47
  61.5 7.9 %collective-permute-start.14 = (bf16[4,96,1024]{2,1,0:T(8,128)(2,1)S(1)}, bf16[4,96,1024]{2,1,0:T(8,128)(2,1)S(1)}, u32[]{:S(2)}, u32[]{:S(2)}) collective-permute-start(bf16[4,96,1024]{2,1,0:T(8,128)(2,1)S(1)} %collective-permute-done.4.s2.refs_2_), channel_id=1, source_target_pairs={{0,16},{1,17},{2,18},{3,19},{4,20},{5,21},{6,22},{7,23},{8,24},{9,... | collective-permute-start | bytes 2359304 | tf_op jit(solution)/shard_map/ppermute | solution.py:47
  63.9 7.0 %collective-permute-start.15 = (bf16[4,96,1024]{2,1,0:T(8,128)(2,1)S(1)}, bf16[4,96,1024]{2,1,0:T(8,128)(2,1)S(1)}, u32[]{:S(2)}, u32[]{:S(2)}) collective-permute-start(bf16[4,96,1024]{2,1,0:T(8,128)(2,1)S(1)} %collective-permute-done.5.s3.refs_3_), channel_id=1, source_target_pairs={{0,16},{1,17},{2,18},{3,19},{4,20},{5,21},{6,22},{7,23},{8,24},{9,... | collective-permute-start | bytes 2359304 | tf_op jit(solution)/shard_map/ppermute | solution.py:47
  65.4 19.0 %collective-permute-start.10 = (bf16[96,1024]{1,0:T(8,128)(2,1)S(1)}, bf16[96,1024]{1,0:T(8,128)(2,1)S(1)}, u32[]{:S(2)}, u32[]{:S(2)}) collective-permute-start(bf16[96,1024]{1,0:T(8,128)(2,1)S(1)} %get-tuple-element.26), channel_id=1, source_target_pairs={{0,2},{1,3},{2,0},{3,1},{4,6},{5,7},{6,4},{7,5},{8,10},{9,11},{10,... | collective-permute-start | bytes 589832 | tf_op jit(solution)/shard_map/ppermute | solution.py:47
  68.8 23.7 %collective-permute-start.11 = (bf16[96,1024]{1,0:T(8,128)(2,1)S(1)}, bf16[96,1024]{1,0:T(8,128)(2,1)S(1)}, u32[]{:S(2)}, u32[]{:S(2)}) collective-permute-start(bf16[96,1024]{1,0:T(8,128)(2,1)S(1)} %get-tuple-element.25), channel_id=1, source_target_pairs={{0,3},{1,0},{2,1},{3,2},{4,7},{5,4},{6,5},{7,6},{8,11},{9,8},{10,9... | collective-permute-start | bytes 589832 | tf_op jit(solution)/shard_map/ppermute | solution.py:47
  69.4 23.1 %collective-permute-start.9 = (bf16[96,1024]{1,0:T(8,128)(2,1)S(1)}, bf16[96,1024]{1,0:T(8,128)(2,1)S(1)}, u32[]{:S(2)}, u32[]{:S(2)}) collective-permute-start(bf16[96,1024]{1,0:T(8,128)(2,1)S(1)} %get-tuple-element.24), channel_id=1, source_target_pairs={{0,1},{1,2},{2,3},{3,0},{4,5},{5,6},{6,7},{7,4},{8,9},{9,10},{10,1... | collective-permute-start | bytes 589832 | tf_op jit(solution)/shard_map/ppermute | solution.py:47
  75.2 18.1 %collective-permute-start.17 = (bf16[192,1536]{1,0:T(8,128)(2,1)S(1)}, bf16[192,1536]{1,0:T(8,128)(2,1)S(1)}, u32[]{:S(2)}, u32[]{:S(2)}) collective-permute-start(bf16[192,1536]{1,0:T(8,128)(2,1)S(1)} %get-tuple-element.18), channel_id=1, source_target_pairs={{0,32},{1,33},{2,34},{3,35},{4,36},{5,37},{6,38},{7,39},{8,40},{9,... | collective-permute-start | bytes 1769480 | tf_op jit(solution)/shard_map/ppermute | solution.py:47
  81.3 22.7 %collective-permute-start.18 = (bf16[192,1536]{1,0:T(8,128)(2,1)S(1)}, bf16[192,1536]{1,0:T(8,128)(2,1)S(1)}, u32[]{:S(2)}, u32[]{:S(2)}) collective-permute-start(bf16[192,1536]{1,0:T(8,128)(2,1)S(1)} %get-tuple-element.19), channel_id=1, source_target_pairs={{0,64},{1,65},{2,66},{3,67},{4,68},{5,69},{6,70},{7,71},{8,72},{9,... | collective-permute-start | bytes 1769480 | tf_op jit(solution)/shard_map/ppermute | solution.py:47
  84.4 23.6 %collective-permute-start.19 = (bf16[192,1536]{1,0:T(8,128)(2,1)S(1)}, bf16[192,1536]{1,0:T(8,128)(2,1)S(1)}, u32[]{:S(2)}, u32[]{:S(2)}) collective-permute-start(bf16[192,1536]{1,0:T(8,128)(2,1)S(1)} %get-tuple-element.20), channel_id=1, source_target_pairs={{0,96},{1,97},{2,98},{3,99},{4,100},{5,101},{6,102},{7,103},{8,104... | collective-permute-start | bytes 1769480 | tf_op jit(solution)/shard_map/ppermute | solution.py:47
  85.8 22.3 %copy-start.4 = (f32[192,1536]{1,0:T(8,128)S(1)}, f32[192,1536]{1,0:T(8,128)}, u32[]{:S(2)}) copy-start(f32[192,1536]{1,0:T(8,128)} %param.10) | copy-start | bytes 3538948
  85.8 22.3 %copy-start.5 = (f32[192,1536]{1,0:T(8,128)S(1)}, f32[192,1536]{1,0:T(8,128)}, u32[]{:S(2)}) copy-start(f32[192,1536]{1,0:T(8,128)} %param.11) | copy-start | bytes 3538948
  85.8 22.3 %copy-start.6 = (f32[192,1536]{1,0:T(8,128)S(1)}, f32[192,1536]{1,0:T(8,128)}, u32[]{:S(2)}) copy-start(f32[192,1536]{1,0:T(8,128)} %param.12) | copy-start | bytes 3538948
  (4 other events, 15.5 us)
